TPU v7x, 32 devices: a whole 2x2x4 slice. The times are simulated.
32 devices in a mesh: dp: 2 (over y), tensor: 16 (over z, x, core).
Axes of the slice: x: 2, y: 2, z: 4, core: 2. Of those that a mesh axis runs over, the one named last changes fastest.
Arguments:
- inputs: float32 [256, 4096], P('dp', 'tensor'), may hold values from -6 to 6
- out_grad: float32 [256, 4096], P('dp', 'tensor'), may hold values from -6 to 6
- up_weight: float32 [768, 128, 128], P('tensor'), may hold values from -0.25 to 0.25
- down_weight: float32 [768, 128, 128], P('tensor'), may hold values from -0.109375 to 0.109375
- up_left: float32 [4096, 128], P('tensor'), may hold values from -0.09375 to 0.09375
- up_right: float32 [128, 16384], P(None, 'tensor'), may hold values from -0.5 to 0.5
- down_left: float32 [16384, 128], P('tensor'), may hold values from -0.046875 to 0.046875
- down_right: float32 [128, 4096], P(None, 'tensor'), may hold values from -0.5 to 0.5
- model_block: int32 [768], P('tensor'), may hold values from 0 to 31, as said below
- hidden_block: int32 [768], P('tensor'), may hold values from 0 to 7
- live_slots: int32 [16], P('tensor'), may hold values from 24 to 48, as said below
Outputs:
- result: float32 [256, 4096], P('dp', 'tensor')
- input_grad: float32 [256, 4096], P('dp', 'tensor')
- up_grad: float32 [768, 128, 128], P('tensor', 'dp')
- down_grad: float32 [768, 128, 128], P('tensor', 'dp')
- up_left_grad: float32 [4096, 128], P(('tensor', 'dp'))
- up_right_grad: float32 [128, 16384], P('dp', 'tensor')
- down_left_grad: float32 [16384, 128], P(('tensor', 'dp'))
- down_right_grad: float32 [128, 4096], P('dp', 'tensor')
Inputs may be any that keep to these rules, and one draw needn't show every extreme that they name: `model_block`: with g the slot's hidden block counted over all owners, the slot's model block differs from g mod 32 in at most one bit. `live_slots`: at least one owner has all 48 slots live.
All inputs are finite; a program needn't handle non-finite values.
Results may differ from a plain program's by a relative error of at most 0.0003.
Values sent between devices are 32-bit elements; how exact they have to be, the bound alone decides.
A program may use at most 64 MiB of HBM per device.

v0:
```python
import jax
import jax.numpy as jnp
from jax import lax
from jax.sharding import PartitionSpec as P

highest = lax.Precision.HIGHEST


def activation(values):
    return jax.nn.gelu(values, approximate=True)


def onehot(indices, extent):
    return (indices[:, None] == jnp.arange(extent, dtype=jnp.int32)[None, :]).astype(jnp.float32)


def spread_cols(field):
    return lax.all_gather(field, "tensor", axis=1, tiled=True)


def rank_total(partial_value):
    return lax.psum(partial_value, "tensor")


def block_total(partial_value):
    return lax.psum_scatter(partial_value, "tensor", scatter_dimension=1, tiled=True)


def shards(
    inputs,
    out_grad,
    up_weight,
    down_weight,
    up_left,
    up_right,
    down_left,
    down_right,
    model_block,
    hidden_block,
    live_slots,
):
    row_count = inputs.shape[0]
    slot_count = up_weight.shape[0]
    block_size = up_weight.shape[1]
    hidden_width = up_right.shape[1]
    local_blocks = hidden_width // block_size
    model_width = inputs.shape[1] * lax.axis_size("tensor")
    model_blocks = model_width // block_size
    alive_mask = (jnp.arange(slot_count, dtype=jnp.int32) < live_slots[0]).astype(jnp.float32)
    up_live = up_weight * alive_mask[:, None, None]
    down_live = down_weight * alive_mask[:, None, None]
    hidden_hot = onehot(hidden_block, local_blocks)
    model_hot = onehot(model_block, model_blocks)
    inputs_full = spread_cols(inputs)
    split_in = inputs_full.reshape(row_count, model_blocks, block_size)
    chosen_in = jnp.take(split_in, model_block, axis=1)
    slot_out = jnp.einsum("tsk,skn->tsn", chosen_in, up_live, precision=highest)
    low_in = rank_total(jnp.dot(inputs, up_left, precision=highest))
    merged = jnp.einsum("tsn,sh->thn", slot_out, hidden_hot, precision=highest)
    preact = merged.reshape(row_count, hidden_width) + jnp.dot(low_in, up_right, precision=highest)
    hidden = activation(preact)
    chosen_hidden = jnp.take(
        hidden.reshape(row_count, local_blocks, block_size), hidden_block, axis=1
    )
    slot_down = jnp.einsum("tsk,skn->tsn", chosen_hidden, down_live, precision=highest)
    placed = jnp.einsum("tsn,sm->tmn", slot_down, model_hot, precision=highest)
    low_mid = rank_total(jnp.dot(hidden, down_left, precision=highest))
    result = block_total(placed.reshape(row_count, model_width)) + jnp.dot(
        low_mid, down_right, precision=highest
    )
    grad_full = spread_cols(out_grad)
    back_mid = rank_total(jnp.dot(out_grad, down_right.T, precision=highest))
    chosen_grad = jnp.take(
        grad_full.reshape(row_count, model_blocks, block_size), model_block, axis=1
    )
    slot_back = jnp.einsum("tsn,skn->tsk", chosen_grad, down_live, precision=highest)
    merged_back = jnp.einsum("tsk,sh->thk", slot_back, hidden_hot, precision=highest)
    hidden_grad = merged_back.reshape(row_count, hidden_width) + jnp.dot(
        back_mid, down_left.T, precision=highest
    )
    _, pullback = jax.vjp(activation, preact)
    preact_grad = pullback(hidden_grad)[0]
    down_grad = (
        jnp.einsum("tsk,tsn->skn", chosen_hidden, chosen_grad, precision=highest)
        * alive_mask[:, None, None]
    )
    down_left_grad = jnp.dot(hidden.T, back_mid, precision=highest)
    down_right_grad = jnp.dot(low_mid.T, out_grad, precision=highest)
    chosen_pgrad = jnp.take(
        preact_grad.reshape(row_count, local_blocks, block_size), hidden_block, axis=1
    )
    slot_in = jnp.einsum("tsn,skn->tsk", chosen_pgrad, up_live, precision=highest)
    placed_in = jnp.einsum("tsk,sm->tmk", slot_in, model_hot, precision=highest)
    back_in = rank_total(jnp.dot(preact_grad, up_right.T, precision=highest))
    input_grad = block_total(placed_in.reshape(row_count, model_width)) + jnp.dot(
        back_in, up_left.T, precision=highest
    )
    up_grad = (
        jnp.einsum("tsk,tsn->skn", chosen_in, chosen_pgrad, precision=highest)
        * alive_mask[:, None, None]
    )
    up_left_grad = jnp.dot(inputs.T, back_in, precision=highest)
    up_right_grad = jnp.dot(low_in.T, preact_grad, precision=highest)
    up_grad, down_grad, up_left_grad, up_right_grad, down_left_grad, down_right_grad = (
        lax.psum_scatter(up_grad, "dp", scatter_dimension=1, tiled=True),
        lax.psum_scatter(down_grad, "dp", scatter_dimension=1, tiled=True),
        lax.psum_scatter(up_left_grad, "dp", scatter_dimension=0, tiled=True),
        lax.psum_scatter(up_right_grad, "dp", scatter_dimension=0, tiled=True),
        lax.psum_scatter(down_left_grad, "dp", scatter_dimension=0, tiled=True),
        lax.psum_scatter(down_right_grad, "dp", scatter_dimension=0, tiled=True),
    )
    return (
        result,
        input_grad,
        up_grad,
        down_grad,
        up_left_grad,
        up_right_grad,
        down_left_grad,
        down_right_grad,
    )


def solution(mesh):
    return jax.shard_map(
        shards,
        mesh=mesh,
        in_specs=(
            P("dp", "tensor"),
            P("dp", "tensor"),
            P("tensor", None, None),
            P("tensor", None, None),
            P("tensor", None),
            P(None, "tensor"),
            P("tensor", None),
            P(None, "tensor"),
            P("tensor"),
            P("tensor"),
            P("tensor"),
        ),
        out_specs=(
            P("dp", "tensor"),
            P("dp", "tensor"),
            P("tensor", "dp", None),
            P("tensor", "dp", None),
            P(("tensor", "dp"), None),
            P("dp", "tensor"),
            P(("tensor", "dp"), None),
            P("dp", "tensor"),
        ),
        check_vma=False,
    )
```

profile of v0, /device:TPU:0, one launch (start us, length us, event | category | flops | bytes accessed | tf_op | source)
XLA Modules:
  0.0 594.8 jit_solution(16330252394450351353)
XLA Ops:
  17.9 37.0 %all-gather.3.cloned.1.call-done = f32[128,4096]{0,1:T(8,128)} async-done(((f32[128,256]{0,1:T(8,128)}), f32[128,4096]{0,1:T(8,128)}) %all-gather.3.cloned.1.call-update) | async-done | bytes 2097168 | tf_op jit(solution)/shard_map/all_gather | solution.py:18
  54.9 1.9 copy.26
  56.9 2.4 gather_fusion
  59.2 10.4 %fusion.26 = f32[128,48,128]{0,2,1:T(8,128)} fusion(f32[48,128,128]{2,1,0:T(8,128)} %gather_fusion, f32[48,128,128]{2,1,0:T(8,128)} %param.17, f32[48]{0:T(128)S(1)} %get-tuple-element.39, pred[48]{0:T(512)(128)(4,1)S(1)} %get-tuple-element.38), kind=kOutput, calls=%fused_computation.32 | convolution fusion | flops 1209532416 | bytes 9437424 | tf_op jit(solution)/shard_map/tsk,skn->tsn/dot_general | solution.py:57
  69.7 3.6 copy.28
  73.3 3.8 fusion.90
  77.1 20.8 %all-gather.5.cloned.1.call-done = f32[128,4096]{0,1:T(8,128)} async-done(((f32[128,256]{0,1:T(8,128)}), f32[128,4096]{0,1:T(8,128)}) %all-gather.5.cloned.1.call-update) | async-done | bytes 2097168 | tf_op jit(solution)/shard_map/all_gather | solution.py:18
  99.8 2.4 gather_fusion.2
  102.2 86.9 %all-reduce.7.cloned.1.call-done = (f32[128,128]{1,0:T(8,128)}, f32[128,128]{1,0:T(8,128)}) async-done(((f32[128,128]{1,0:T(8,128)}, f32[128,128]{1,0:T(8,128)}), (f32[128,128]{1,0:T(8,128)}, f32[128,128]{1,0:T(8,128)})) %all-reduce.7.cloned.1.call-update) | async-done | bytes 131088 | tf_op jit(solution)/shard_map/psum | solution.py:22
  192.6 9.8 %fusion.36 = f32[128,48,128]{0,2,1:T(8,128)} fusion(f32[48,128,128]{2,1,0:T(8,128)S(1)} %copy-done.2, f32[48,128,128]{2,1,0:T(8,128)} %param.18, f32[48]{0:T(128)S(1)} %get-tuple-element.39, pred[48]{0:T(512)(128)(4,1)S(1)} %get-tuple-element.38), kind=kOutput, calls=%fused_computation.34 | convolution fusion | flops 1209532416 | bytes 9437424 | tf_op jit(solution)/shard_map/tsn,skn->tsk/dot_general | solution.py:76
  202.4 3.6 copy.34
  206.0 3.0 fusion.88
  211.2 2.5 gather_fusion.1
  213.8 10.4 %fusion.31 = f32[128,48,128]{0,2,1:T(8,128)} fusion(f32[48,128,128]{2,1,0:T(8,128)} %gather_fusion.1, f32[48,128,128]{2,1,0:T(8,128)} %param.18, f32[48]{0:T(128)S(1)} %get-tuple-element.39, pred[48]{0:T(512)(128)(4,1)S(1)} %compare_and_fusion), kind=kOutput, calls=%fused_computation.33 | convolution fusion | flops 1209532416 | bytes 9437424 | tf_op jit(solution)/shard_map/tsk,skn->tsn/dot_general | solution.py:65
  224.2 3.8 copy.31
  228.0 75.9 %all-reduce.5.cloned.1.call-done = (f32[128,128]{1,0:T(8,128)}, f32[128,128]{1,0:T(8,128)}) async-done(((f32[128,128]{1,0:T(8,128)}, f32[128,128]{1,0:T(8,128)}), (f32[128,128]{1,0:T(8,128)}, f32[128,128]{1,0:T(8,128)})) %all-reduce.5.cloned.1.call-update) | async-done | bytes 131088 | tf_op jit(solution)/shard_map/psum | solution.py:22
  305.8 3.2 fusion.83
  309.0 2.9 copy.59
  312.0 2.4 gather_fusion.3
  314.5 11.2 %fusion.41 = f32[128,48,128]{0,2,1:T(8,128)} fusion(f32[48,128,128]{2,1,0:T(8,128)} %gather_fusion.3, f32[48,128,128]{2,1,0:T(8,128)} %param.17, f32[48]{0:T(128)S(1)} %get-tuple-element.39, pred[48]{0:T(512)(128)(4,1)S(1)} %compare_and_fusion), kind=kOutput, calls=%fused_computation.35 | convolution fusion | flops 1209532416 | bytes 9437424 | tf_op jit(solution)/shard_map/tsn,skn->tsk/dot_general | solution.py:92
  325.7 4.1 copy.36
  329.7 3.3 fusion.81
  333.0 3.0 copy.58
  340.6 10.0 %fusion.46 = f32[48,128,128]{2,1,0:T(8,128)} fusion(f32[48,128,128]{2,1,0:T(8,128)} %gather_fusion.2, f32[48,128,128]{2,1,0:T(8,128)} %gather_fusion.1, f32[48]{0:T(128)S(1)} %get-tuple-element.39, pred[48]{0:T(512)(128)(4,1)S(1)} %compare_and_fusion, pred[48]{0:T(512)(128)(4,1)S(1)} %get-tuple-element.38), kind=kOutput, calls=%fused_computation.36 | convolution fusion | flops 1210318848 | bytes 9437472 | tf_op jit(solution)/shard_map/tsk,tsn->skn/dot_general | solution.py:84
  350.9 10.0 %fusion.51 = f32[48,128,128]{2,1,0:T(8,128)} fusion(f32[48,128,128]{2,1,0:T(8,128)} %gather_fusion.3, f32[48,128,128]{2,1,0:T(8,128)} %gather_fusion, f32[48]{0:T(128)S(1)} %get-tuple-element.39, pred[48]{0:T(512)(128)(4,1)S(1)} %compare_and_fusion, pred[48]{0:T(512)(128)(4,1)S(1)} %get-tuple-element.38), kind=kOutput, calls=%fused_computation.37 | convolution fusion | flops 1210318848 | bytes 9437472 | tf_op jit(solution)/shard_map/tsk,tsn->skn/dot_general | solution.py:99
  362.6 21.3 %reduce-scatter.9.cloned.1.call-done = f32[128,256]{1,0:T(8,128)} async-done(((f32[128,4096]{1,0:T(8,128)}), f32[128,256]{1,0:T(8,128)}) %reduce-scatter.9.cloned.1.call-update) | async-done | bytes 131088 | tf_op jit(solution)/shard_map/reduce_scatter | solution.py:26
  385.7 62.7 %reduce-scatter.11.cloned.1.call-done = f32[128,256]{1,0:T(8,128)} async-done(((f32[128,4096]{1,0:T(8,128)}), f32[128,256]{1,0:T(8,128)}) %reduce-scatter.11.cloned.1.call-update) | async-done | bytes 131088 | tf_op jit(solution)/shard_map/reduce_scatter | solution.py:26
  450.2 10.3 %reduce-scatter.23.cloned.1.call-done = f32[64,256]{1,0:T(8,128)} async-done(((f32[128,256]{1,0:T(8,128)}), f32[64,256]{1,0:T(8,128)}) %reduce-scatter.23.cloned.1.call-update) | async-done | bytes 65552 | tf_op jit(solution)/shard_map/reduce_scatter | solution.py:110
  460.5 17.5 %reduce-scatter.21.cloned.1.call-done = f32[512,128]{1,0:T(8,128)} async-done(((f32[1024,128]{1,0:T(8,128)}), f32[512,128]{1,0:T(8,128)}) %reduce-scatter.21.cloned.1.call-update) | async-done | bytes 262160 | tf_op jit(solution)/shard_map/reduce_scatter | solution.py:109
  478.0 17.3 %reduce-scatter.19.cloned.1.call-done = f32[64,1024]{1,0:T(8,128)} async-done(((f32[128,1024]{1,0:T(8,128)}), f32[64,1024]{1,0:T(8,128)}) %reduce-scatter.19.cloned.1.call-update) | async-done | bytes 262160 | tf_op jit(solution)/shard_map/reduce_scatter | solution.py:108
  495.3 46.3 %reduce-scatter.15.cloned.1.call-done = f32[48,64,128]{2,1,0:T(8,128)} async-done(((f32[48,128,128]{2,1,0:T(8,128)}), f32[48,64,128]{2,1,0:T(8,128)}) %reduce-scatter.15.cloned.1.call-update) | async-done | bytes 1572880 | tf_op jit(solution)/shard_map/reduce_scatter | solution.py:106
  541.6 46.1 %reduce-scatter.13.cloned.1.call-done = f32[48,64,128]{2,1,0:T(8,128)} async-done(((f32[48,128,128]{2,1,0:T(8,128)}), f32[48,64,128]{2,1,0:T(8,128)}) %reduce-scatter.13.cloned.1.call-update) | async-done | bytes 1572880 | tf_op jit(solution)/shard_map/reduce_scatter | solution.py:105
  (77 shorter events, 29.7 us)
Async XLA Ops:
  7.2 184.0 %copy-start = (f32[1024,128]{1,0:T(8,128)S(1)}, f32[1024,128]{1,0:T(8,128)}, u32[]{:S(2)}) copy-start(f32[1024,128]{1,0:T(8,128)} %param.21) | copy-start | bytes 1572868
  7.2 47.8 %all-gather.3.cloned.1.call-start = ((), (), s32[]{:S(2)}) async-start(), calls=%async_computation.8 | async-start | bytes 2228224 | tf_op jit(solution)/shard_map/all_gather | solution.py:18
  9.0 88.9 %all-gather.5.cloned.1.call-start = ((), (), s32[]{:S(2)}) async-start(), calls=%async_computation.10 | async-start | bytes 2228224 | tf_op jit(solution)/shard_map/all_gather | solution.py:18
  10.7 178.4 %all-reduce.7.cloned.1.call-start = ((), (), s32[]{:S(2)}) async-start(), calls=%async_computation.19 | async-start | bytes 262144 | tf_op jit(solution)/shard_map/psum | solution.py:22
  14.5 289.3 %all-reduce.5.cloned.1.call-start = ((), (), s32[]{:S(2)}) async-start(), calls=%async_computation.18 | async-start | bytes 262144 | tf_op jit(solution)/shard_map/psum | solution.py:22
  69.7 3.6 copy-start.12
  99.8 89.3 %copy-start.3 = (f32[128,1024]{1,0:T(8,128)S(1)}, f32[128,1024]{1,0:T(8,128)}, u32[]{:S(2)}) copy-start(f32[128,1024]{1,0:T(8,128)} %param.20) | copy-start | bytes 1572868
  189.1 3.5 copy-start.2
  206.0 3.0 copy-start.13
  213.7 147.2 %reduce-scatter.17.cloned.1.call-start = ((), (), s32[]{:S(2)}) async-start(), calls=%async_computation.14 | async-start | bytes 196608 | tf_op jit(solution)/shard_map/reduce_scatter | solution.py:107
  224.2 79.7 %copy-start.4 = (f32[128,256]{1,0:T(8,128)S(1)}, f32[128,256]{1,0:T(8,128)}, u32[]{:S(2)}) copy-start(f32[128,256]{1,0:T(8,128)} %param.15) | copy-start | bytes 393220
  224.2 81.6 %copy-start.11 = (s32[48]{0:T(128)S(1)}, s32[48]{0:T(128)}, u32[]{:S(2)}) copy-start(s32[48]{0:T(128)} %param.23) | copy-start | bytes 580
  305.7 78.2 %reduce-scatter.9.cloned.1.call-start = ((), (), s32[]{:S(2)}) async-start(), calls=%async_computation.9 | async-start | bytes 2228224 | tf_op jit(solution)/shard_map/reduce_scatter | solution.py:26
  311.9 136.5 %reduce-scatter.11.cloned.1.call-start = ((), (), s32[]{:S(2)}) async-start(), calls=%async_computation.11 | async-start | bytes 2228224 | tf_op jit(solution)/shard_map/reduce_scatter | solution.py:26
  333.0 3.1 copy-start.5
  333.0 3.1 copy-start.10
  336.0 3.1 copy-start.8
  336.0 124.5 %reduce-scatter.23.cloned.1.call-start = ((), (), s32[]{:S(2)}) async-start(), calls=%async_computation.17 | async-start | bytes 196608 | tf_op jit(solution)/shard_map/reduce_scatter | solution.py:110
  337.1 140.9 %reduce-scatter.21.cloned.1.call-start = ((), (), s32[]{:S(2)}) async-start(), calls=%async_computation.16 | async-start | bytes 786432 | tf_op jit(solution)/shard_map/reduce_scatter | solution.py:109
  339.1 156.3 %reduce-scatter.19.cloned.1.call-start = ((), (), s32[]{:S(2)}) async-start(), calls=%async_computation.15 | async-start | bytes 786432 | tf_op jit(solution)/shard_map/reduce_scatter | solution.py:108
  340.6 201.1 %reduce-scatter.15.cloned.1.call-start = ((), (), s32[]{:S(2)}) async-start(), calls=%async_computation.13 | async-start | bytes 4718592 | tf_op jit(solution)/shard_map/reduce_scatter | solution.py:106
  350.6 237.1 %reduce-scatter.13.cloned.1.call-start = ((), (), s32[]{:S(2)}) async-start(), calls=%async_computation.12 | async-start | bytes 4718592 | tf_op jit(solution)/shard_map/reduce_scatter | solution.py:105
  350.9 236.9 %copy-start.1 = (f32[1024,128]{1,0:T(8,128)S(1)}, f32[1024,128]{1,0:T(8,128)}, u32[]{:S(2)}) copy-start(f32[1024,128]{1,0:T(8,128)} %param.21) | copy-start | bytes 1572868
  360.9 23.0 %copy-start.6 = (f32[128,256]{1,0:T(8,128)S(1)}, f32[128,256]{1,0:T(8,128)}, u32[]{:S(2)}) copy-start(f32[128,256]{1,0:T(8,128)} %param.22) | copy-start | bytes 393220
  360.9 87.5 %copy-start.7 = (f32[256,128]{1,0:T(8,128)S(1)}, f32[256,128]{1,0:T(8,128)}, u32[]{:S(2)}) copy-start(f32[256,128]{1,0:T(8,128)} %param.19) | copy-start | bytes 393220
  360.9 87.5 %copy-start.9 = (f32[128,128]{1,0:T(8,128)S(1)}, f32[128,128]{1,0:T(8,128)}, u32[]{:S(2)}) copy-start(f32[128,128]{1,0:T(8,128)} %get-tuple-element.35) | copy-start | bytes 196612
Sparse Core Ops, SparseCore 0:
  10.7 44.1 all-gather.2
  57.7 40.1 all-gather.4
  102.0 87.0 all-reduce.6
  213.8 89.9 all-reduce.4
  306.5 12.0 reduce-scatter.16
  322.1 61.7 reduce-scatter.8
  387.7 60.6 reduce-scatter.10
  451.2 9.3 reduce-scatter.22
  463.4 14.6 reduce-scatter.20
  480.7 14.6 reduce-scatter.18
  498.2 43.4 reduce-scatter.14
  544.3 43.4 reduce-scatter.12
where the time goes:
time: 603 us; the launch traced here: 595 us
  waiting for transfers between devices  442 us (73%)
  matrix products  94.1 us (16%)
  local copies, waits for them, and re-layouts  39.8 us (7%)
  between operations  15.2 us (3%)
    psum x2, waiting for transfers between devices, rank_total(): return lax.psum(partial_value, 'tensor')  163 us
    reduce_scatter x2, waiting for transfers between devices, block_total(): lax.psum_scatter(partial_value, 'tensor', scatter_dimension=1, tiled=True)  83.9 us
    all_gather x2, waiting for transfers between devices, spread_cols(): return lax.all_gather(field, 'tensor', axis=1, tiled=True)  57.8 us
    reduce_scatter x1, waiting for transfers between devices, shards(): lax.psum_scatter(down_grad, 'dp', scatter_dimension=1, tiled=True)  46.3 us
    reduce_scatter x1, waiting for transfers between devices, shards(): lax.psum_scatter(up_grad, 'dp', scatter_dimension=1, tiled=True)  46.1 us
    reduce_scatter x1, waiting for transfers between devices, shards(): lax.psum_scatter(down_left_grad, 'dp', scatter_dimension=0, tiled=True)  17.5 us
    reduce_scatter x1, waiting for transfers between devices, shards(): lax.psum_scatter(up_right_grad, 'dp', scatter_dimension=0, tiled=True)  17.3 us
  transfers between devices with their start and end apart: 12, of which 11 were waited for; matrix products, arithmetic and copies ran while one was open for 18% of the time, Pallas kernels for 0%

commit v1 on v0

--- a/solution.py
+++ b/solution.py
@@ -4,6 +4,22 @@
 from jax.sharding import PartitionSpec as P
 
 highest = lax.Precision.HIGHEST
+
+
+def gather_around(x, axis, dim):
+    ways, here, step = (lax.axis_size(axis), lax.axis_index(axis), x.shape[dim])
+    lengths = [n * ways if d == dim else n for d, n in enumerate(x.shape)]
+    full = lax.dynamic_update_slice_in_dim(jnp.zeros(lengths, x.dtype), x, here * step, axis=dim)
+    going_up = going_down = x
+    for far in range(1, ways // 2 + 1):
+        going_up = lax.ppermute(going_up, axis, [(d, (d + 1) % ways) for d in range(ways)])
+        full = lax.dynamic_update_slice_in_dim(full, going_up, (here - far) % ways * step, axis=dim)
+        if 2 * far < ways:
+            going_down = lax.ppermute(going_down, axis, [(d, (d - 1) % ways) for d in range(ways)])
+            full = lax.dynamic_update_slice_in_dim(
+                full, going_down, (here + far) % ways * step, axis=dim
+            )
+    return full
 
 
 def activation(values):
@@ -15,7 +31,7 @@
 
 
 def spread_cols(field):
-    return lax.all_gather(field, "tensor", axis=1, tiled=True)
+    return gather_around(field, "tensor", 1)
 
 
 def rank_total(partial_value):

time: 603 us -> 529 us (0.88)
  waiting for transfers between devices: 442 us -> 305 us
  starting transfers between devices: 0.67 us -> 65 us
    psum x2, waiting for transfers between devices: 163 us -> 68.4 us  [rank_total(): return lax.psum(partial_value, 'tensor')]
    ppermute x0 -> x30, starting transfers between devices: none -> 63.8 us  [the longest x14 63.6 us: gather_around(): lax.ppermute(going_down, axis, [(d, (d - 1) % ways) for d in range(ways)])]
    all_gather x2 -> x0, waiting for transfers between devices: 57.8 us -> none  [spread_cols(): return lax.all_gather(field, 'tensor', axis=1, tiled=True)]
    ppermute x0 -> x30, waiting for transfers between devices: none -> 14.1 us  [the longest x16 14 us: gather_around(): lax.ppermute(going_up, axis, [(d, (d + 1) % ways) for d in range(ways)])]
  transfers between devices with their start and end apart: 12 -> 40, of which waited for: 11 -> 12; matrix products, arithmetic and copies ran while one was open for 18% -> 24% of each run, Pallas kernels for 0% -> 0%
where the time goes in v1:
time: 529 us; the launch traced here: 525 us
  waiting for transfers between devices  305 us (58%)
  matrix products  93.5 us (18%)
  starting transfers between devices  65 us (12%)
  local copies, waits for them, and re-layouts  43.5 us (8%)
  between operations  16 us (3%)
    reduce_scatter x2, waiting for transfers between devices, block_total(): lax.psum_scatter(partial_value, 'tensor', scatter_dimension=1, tiled=True)  84.3 us
    psum x2, waiting for transfers between devices, rank_total(): return lax.psum(partial_value, 'tensor')  68.4 us
    ppermute x14, starting transfers between devices, gather_around(): lax.ppermute(going_down, axis, [(d, (d - 1) % ways) for d in range(ways)])  63.6 us
    reduce_scatter x1, waiting for transfers between devices, shards(): lax.psum_scatter(up_grad, 'dp', scatter_dimension=1, tiled=True)  46.3 us
    reduce_scatter x1, waiting for transfers between devices, shards(): lax.psum_scatter(down_grad, 'dp', scatter_dimension=1, tiled=True)  46.1 us
    reduce_scatter x1, waiting for transfers between devices, shards(): lax.psum_scatter(up_right_grad, 'dp', scatter_dimension=0, tiled=True)  17.5 us
    reduce_scatter x1, waiting for transfers between devices, shards(): lax.psum_scatter(down_left_grad, 'dp', scatter_dimension=0, tiled=True)  17.5 us
    ppermute x16, waiting for transfers between devices, gather_around(): lax.ppermute(going_up, axis, [(d, (d + 1) % ways) for d in range(ways)])  14 us
  transfers between devices with their start and end apart: 40, of which 12 were waited for; matrix products, arithmetic and copies ran while one was open for 24% of the time, Pallas kernels for 0%

profile of v1, /device:TPU:0, one launch (start us, length us, event | category | flops | bytes accessed | tf_op | source)
XLA Modules:
  0.0 524.7 jit_solution(2298526887249098254)
XLA Ops:
  8.3 5.5 %collective-permute-start.16 = (f32[128,256]{0,1:T(8,128)S(1)}, f32[128,256]{0,1:T(8,128)S(1)}, u32[]{:S(2)}, u32[]{:S(2)}) collective-permute-start(f32[128,256]{0,1:T(8,128)S(1)} %copy.34), channel_id=1, source_target_pairs={{0,15},{1,0},{2,1},{3,2},{4,3},{5,4},{6,5},{7,6},{8,7},{9,8},{10,9... | collective-permute-start | bytes 393224 | tf_op jit(solution)/shard_map/ppermute | solution.py:18
  14.8 4.5 collective-permute-start.1
  26.4 4.5 collective-permute-start.18
  30.9 4.4 collective-permute-start.3
  35.5 4.5 collective-permute-start.20
  40.0 4.4 collective-permute-start.5
  44.5 4.5 collective-permute-start.22
  49.0 4.4 collective-permute-start.7
  53.6 4.5 collective-permute-start.24
  58.1 4.4 collective-permute-start.9
  62.6 4.5 collective-permute-start.26
  67.1 4.4 collective-permute-start.11
  71.7 4.5 collective-permute-start.28
  76.2 4.4 collective-permute-start.13
  83.3 4.5 collective-permute-done.12
  90.4 4.6 collective-permute-done.14
  101.9 4.0 gather_fusion
  108.3 11.3 %fusion.36 = f32[128,48,128]{0,2,1:T(8,128)} fusion(f32[48,128,128]{2,1,0:T(8,128)} %gather_fusion.2, f32[48,128,128]{2,1,0:T(8,128)} %param.18, f32[48]{0:T(128)S(1)} %compare_convert_fusion, pred[48]{0:T(512)(128)(4,1)S(1)} %get-tuple-element.39), kind=kOutput, calls=%fused_computation.34 | convolution fusion | flops 1209532416 | bytes 9437424 | tf_op jit(solution)/shard_map/tsn,skn->tsk/dot_general | solution.py:92
  126.4 8.5 %fusion.26 = f32[128,48,128]{0,2,1:T(8,128)} fusion(f32[48,128,128]{2,1,0:T(8,128)S(1)} %copy-done.2, f32[48,128,128]{2,1,0:T(8,128)} %param.17, f32[48]{0:T(128)S(1)} %compare_convert_fusion, pred[48]{0:T(512)(128)(4,1)S(1)} %get-tuple-element.39), kind=kOutput, calls=%fused_computation.32 | convolution fusion | flops 1209532416 | bytes 9437424 | tf_op jit(solution)/shard_map/tsk,skn->tsn/dot_general | solution.py:73
  135.0 3.8 copy.30
  150.4 11.2 %fusion.41 = f32[128,48,128]{0,2,1:T(8,128)} fusion(f32[48,128,128]{2,1,0:T(8,128)} %gather_fusion.3, f32[48,128,128]{2,1,0:T(8,128)} %param.17, f32[48]{0:T(128)S(1)} %compare_convert_fusion, pred[48]{0:T(512)(128)(4,1)S(1)} %get-tuple-element.38), kind=kOutput, calls=%fused_computation.35 | convolution fusion | flops 1209532416 | bytes 9437424 | tf_op jit(solution)/shard_map/tsn,skn->tsk/dot_general | solution.py:108
  165.3 68.4 %all-reduce.5.cloned.1.call-done = (f32[128,128]{1,0:T(8,128)}, f32[128,128]{1,0:T(8,128)}) async-done(((f32[128,128]{1,0:T(8,128)}, f32[128,128]{1,0:T(8,128)}), (f32[128,128]{1,0:T(8,128)}, f32[128,128]{1,0:T(8,128)})) %all-reduce.5.cloned.1.call-update) | async-done | bytes 131088 | tf_op jit(solution)/shard_map/psum | solution.py:38
  244.9 10.4 %fusion.31 = f32[128,48,128]{0,2,1:T(8,128)} fusion(f32[48,128,128]{2,1,0:T(8,128)} %gather_fusion.1, f32[48,128,128]{2,1,0:T(8,128)} %param.18, f32[48]{0:T(128)S(1)} %compare_convert_fusion, pred[48]{0:T(512)(128)(4,1)S(1)} %get-tuple-element.38), kind=kOutput, calls=%fused_computation.33 | convolution fusion | flops 1209532416 | bytes 9437424 | tf_op jit(solution)/shard_map/tsk,skn->tsn/dot_general | solution.py:81
  270.0 10.0 %fusion.51 = f32[48,128,128]{2,1,0:T(8,128)} fusion(f32[48,128,128]{2,1,0:T(8,128)} %gather_fusion.3, f32[48,128,128]{2,1,0:T(8,128)} %gather_fusion, f32[48]{0:T(128)S(1)} %compare_convert_fusion, pred[48]{0:T(512)(128)(4,1)S(1)} %get-tuple-element.38, pred[48]{0:T(512)(128)(4,1)S(1)} %get-tuple-element.39), kind=kOutput, calls=%fused_computation.37 | convolution fusion | flops 1210318848 | bytes 9437472 | tf_op jit(solution)/shard_map/tsk,tsn->skn/dot_general | solution.py:115
  280.3 10.1 %fusion.46 = f32[48,128,128]{2,1,0:T(8,128)} fusion(f32[48,128,128]{2,1,0:T(8,128)} %gather_fusion.2, f32[48,128,128]{2,1,0:T(8,128)} %gather_fusion.1, f32[48]{0:T(128)S(1)} %compare_convert_fusion, pred[48]{0:T(512)(128)(4,1)S(1)} %get-tuple-element.38, pred[48]{0:T(512)(128)(4,1)S(1)} %get-tuple-element.39), kind=kOutput, calls=%fused_computation.36 | convolution fusion | flops 1210318848 | bytes 9437472 | tf_op jit(solution)/shard_map/tsk,tsn->skn/dot_general | solution.py:100
  292.1 21.9 %reduce-scatter.11.cloned.1.call-done = f32[128,256]{1,0:T(8,128)} async-done(((f32[128,4096]{1,0:T(8,128)}), f32[128,256]{1,0:T(8,128)}) %reduce-scatter.11.cloned.1.call-update) | async-done | bytes 131088 | tf_op jit(solution)/shard_map/reduce_scatter | solution.py:42
  315.8 62.5 %reduce-scatter.9.cloned.1.call-done = f32[128,256]{1,0:T(8,128)} async-done(((f32[128,4096]{1,0:T(8,128)}), f32[128,256]{1,0:T(8,128)}) %reduce-scatter.9.cloned.1.call-update) | async-done | bytes 131088 | tf_op jit(solution)/shard_map/reduce_scatter | solution.py:42
  380.1 10.1 %reduce-scatter.23.cloned.1.call-done = f32[64,256]{1,0:T(8,128)} async-done(((f32[128,256]{1,0:T(8,128)}), f32[64,256]{1,0:T(8,128)}) %reduce-scatter.23.cloned.1.call-update) | async-done | bytes 65552 | tf_op jit(solution)/shard_map/reduce_scatter | solution.py:126
  390.2 17.5 %reduce-scatter.21.cloned.1.call-done = f32[512,128]{1,0:T(8,128)} async-done(((f32[1024,128]{1,0:T(8,128)}), f32[512,128]{1,0:T(8,128)}) %reduce-scatter.21.cloned.1.call-update) | async-done | bytes 262160 | tf_op jit(solution)/shard_map/reduce_scatter | solution.py:125
  407.7 17.5 %reduce-scatter.19.cloned.1.call-done = f32[64,1024]{1,0:T(8,128)} async-done(((f32[128,1024]{1,0:T(8,128)}), f32[64,1024]{1,0:T(8,128)}) %reduce-scatter.19.cloned.1.call-update) | async-done | bytes 262160 | tf_op jit(solution)/shard_map/reduce_scatter | solution.py:124
  425.2 46.3 %reduce-scatter.13.cloned.1.call-done = f32[48,64,128]{2,1,0:T(8,128)} async-done(((f32[48,128,128]{2,1,0:T(8,128)}), f32[48,64,128]{2,1,0:T(8,128)}) %reduce-scatter.13.cloned.1.call-update) | async-done | bytes 1572880 | tf_op jit(solution)/shard_map/reduce_scatter | solution.py:121
  471.5 46.1 %reduce-scatter.15.cloned.1.call-done = f32[48,64,128]{2,1,0:T(8,128)} async-done(((f32[48,128,128]{2,1,0:T(8,128)}), f32[48,64,128]{2,1,0:T(8,128)}) %reduce-scatter.15.cloned.1.call-update) | async-done | bytes 1572880 | tf_op jit(solution)/shard_map/reduce_scatter | solution.py:122
  (168 shorter events, 76.5 us)
Async XLA Ops:
  7.2 134.7 %all-reduce.7.cloned.1.call-start = ((), (), s32[]{:S(2)}) async-start(), calls=%async_computation.17 | async-start | bytes 262144 | tf_op jit(solution)/shard_map/psum | solution.py:38
  8.3 18.2 %collective-permute-start.16 = (f32[128,256]{0,1:T(8,128)S(1)}, f32[128,256]{0,1:T(8,128)S(1)}, u32[]{:S(2)}, u32[]{:S(2)}) collective-permute-start(f32[128,256]{0,1:T(8,128)S(1)} %copy.34), channel_id=1, source_target_pairs={{0,15},{1,0},{2,1},{3,2},{4,3},{5,4},{6,5},{7,6},{8,7},{9,8},{10,9... | collective-permute-start | bytes 393224 | tf_op jit(solution)/shard_map/ppermute | solution.py:18
  13.8 17.2 %collective-permute-start.15 = (f32[128,256]{0,1:T(8,128)S(1)}, f32[128,256]{0,1:T(8,128)S(1)}, u32[]{:S(2)}, u32[]{:S(2)}) collective-permute-start(f32[128,256]{0,1:T(8,128)S(1)} %copy.34), channel_id=1, source_target_pairs={{0,1},{1,2},{2,3},{3,4},{4,5},{5,6},{6,7},{7,8},{8,9},{9,10},{10,1... | collective-permute-start | bytes 393224 | tf_op jit(solution)/shard_map/ppermute | solution.py:15
  14.8 16.2 %collective-permute-start.1 = (f32[128,256]{0,1:T(8,128)S(1)}, f32[128,256]{0,1:T(8,128)S(1)}, u32[]{:S(2)}, u32[]{:S(2)}) collective-permute-start(f32[128,256]{0,1:T(8,128)S(1)} %copy.25), channel_id=1, source_target_pairs={{0,15},{1,0},{2,1},{3,2},{4,3},{5,4},{6,5},{7,6},{8,7},{9,8},{10,9... | collective-permute-start | bytes 393224 | tf_op jit(solution)/shard_map/ppermute | solution.py:18
  19.3 16.1 %collective-permute-start = (f32[128,256]{0,1:T(8,128)S(1)}, f32[128,256]{0,1:T(8,128)S(1)}, u32[]{:S(2)}, u32[]{:S(2)}) collective-permute-start(f32[128,256]{0,1:T(8,128)S(1)} %copy.25), channel_id=1, source_target_pairs={{0,1},{1,2},{2,3},{3,4},{4,5},{5,6},{6,7},{7,8},{8,9},{9,10},{10,1... | collective-permute-start | bytes 393224 | tf_op jit(solution)/shard_map/ppermute | solution.py:15
  23.0 210.7 %all-reduce.5.cloned.1.call-start = ((), (), s32[]{:S(2)}) async-start(), calls=%async_computation.16 | async-start | bytes 262144 | tf_op jit(solution)/shard_map/psum | solution.py:38
  30.9 9.0 %collective-permute-start.17 = (f32[128,256]{0,1:T(8,128)S(1)}, f32[128,256]{0,1:T(8,128)S(1)}, u32[]{:S(2)}, u32[]{:S(2)}) collective-permute-start(f32[128,256]{0,1:T(8,128)S(1)} %collective-permute-done.15), channel_id=1, source_target_pairs={{0,1},{1,2},{2,3},{3,4},{4,5},{5,6},{6,7},{7,8},{8,9},{9,10},{10,1... | collective-permute-start | bytes 393224 | tf_op jit(solution)/shard_map/ppermute | solution.py:15
  30.9 9.0 %collective-permute-start.3 = (f32[128,256]{0,1:T(8,128)S(1)}, f32[128,256]{0,1:T(8,128)S(1)}, u32[]{:S(2)}, u32[]{:S(2)}) collective-permute-start(f32[128,256]{0,1:T(8,128)S(1)} %collective-permute-done.1), channel_id=1, source_target_pairs={{0,15},{1,0},{2,1},{3,2},{4,3},{5,4},{6,5},{7,6},{8,7},{9,8},{10,9... | collective-permute-start | bytes 393224 | tf_op jit(solution)/shard_map/ppermute | solution.py:18
  35.4 9.0 %collective-permute-start.2 = (f32[128,256]{0,1:T(8,128)S(1)}, f32[128,256]{0,1:T(8,128)S(1)}, u32[]{:S(2)}, u32[]{:S(2)}) collective-permute-start(f32[128,256]{0,1:T(8,128)S(1)} %collective-permute-done), channel_id=1, source_target_pairs={{0,1},{1,2},{2,3},{3,4},{4,5},{5,6},{6,7},{7,8},{8,9},{9,10},{10,1... | collective-permute-start | bytes 393224 | tf_op jit(solution)/shard_map/ppermute | solution.py:15
  40.0 9.0 %collective-permute-start.19 = (f32[128,256]{0,1:T(8,128)S(1)}, f32[128,256]{0,1:T(8,128)S(1)}, u32[]{:S(2)}, u32[]{:S(2)}) collective-permute-start(f32[128,256]{0,1:T(8,128)S(1)} %collective-permute-done.17), channel_id=1, source_target_pairs={{0,1},{1,2},{2,3},{3,4},{4,5},{5,6},{6,7},{7,8},{8,9},{9,10},{10,1... | collective-permute-start | bytes 393224 | tf_op jit(solution)/shard_map/ppermute | solution.py:15
  40.0 9.0 %collective-permute-start.5 = (f32[128,256]{0,1:T(8,128)S(1)}, f32[128,256]{0,1:T(8,128)S(1)}, u32[]{:S(2)}, u32[]{:S(2)}) collective-permute-start(f32[128,256]{0,1:T(8,128)S(1)} %collective-permute-done.3), channel_id=1, source_target_pairs={{0,15},{1,0},{2,1},{3,2},{4,3},{5,4},{6,5},{7,6},{8,7},{9,8},{10,9... | collective-permute-start | bytes 393224 | tf_op jit(solution)/shard_map/ppermute | solution.py:18
  44.4 9.0 %collective-permute-start.4 = (f32[128,256]{0,1:T(8,128)S(1)}, f32[128,256]{0,1:T(8,128)S(1)}, u32[]{:S(2)}, u32[]{:S(2)}) collective-permute-start(f32[128,256]{0,1:T(8,128)S(1)} %collective-permute-done.2), channel_id=1, source_target_pairs={{0,1},{1,2},{2,3},{3,4},{4,5},{5,6},{6,7},{7,8},{8,9},{9,10},{10,1... | collective-permute-start | bytes 393224 | tf_op jit(solution)/shard_map/ppermute | solution.py:15
  49.0 9.0 %collective-permute-start.21 = (f32[128,256]{0,1:T(8,128)S(1)}, f32[128,256]{0,1:T(8,128)S(1)}, u32[]{:S(2)}, u32[]{:S(2)}) collective-permute-start(f32[128,256]{0,1:T(8,128)S(1)} %collective-permute-done.19), channel_id=1, source_target_pairs={{0,1},{1,2},{2,3},{3,4},{4,5},{5,6},{6,7},{7,8},{8,9},{9,10},{10,1... | collective-permute-start | bytes 393224 | tf_op jit(solution)/shard_map/ppermute | solution.py:15
  49.0 9.0 %collective-permute-start.7 = (f32[128,256]{0,1:T(8,128)S(1)}, f32[128,256]{0,1:T(8,128)S(1)}, u32[]{:S(2)}, u32[]{:S(2)}) collective-permute-start(f32[128,256]{0,1:T(8,128)S(1)} %collective-permute-done.5), channel_id=1, source_target_pairs={{0,15},{1,0},{2,1},{3,2},{4,3},{5,4},{6,5},{7,6},{8,7},{9,8},{10,9... | collective-permute-start | bytes 393224 | tf_op jit(solution)/shard_map/ppermute | solution.py:18
  53.5 9.0 %collective-permute-start.6 = (f32[128,256]{0,1:T(8,128)S(1)}, f32[128,256]{0,1:T(8,128)S(1)}, u32[]{:S(2)}, u32[]{:S(2)}) collective-permute-start(f32[128,256]{0,1:T(8,128)S(1)} %collective-permute-done.4), channel_id=1, source_target_pairs={{0,1},{1,2},{2,3},{3,4},{4,5},{5,6},{6,7},{7,8},{8,9},{9,10},{10,1... | collective-permute-start | bytes 393224 | tf_op jit(solution)/shard_map/ppermute | solution.py:15
  58.1 9.0 %collective-permute-start.23 = (f32[128,256]{0,1:T(8,128)S(1)}, f32[128,256]{0,1:T(8,128)S(1)}, u32[]{:S(2)}, u32[]{:S(2)}) collective-permute-start(f32[128,256]{0,1:T(8,128)S(1)} %collective-permute-done.21), channel_id=1, source_target_pairs={{0,1},{1,2},{2,3},{3,4},{4,5},{5,6},{6,7},{7,8},{8,9},{9,10},{10,1... | collective-permute-start | bytes 393224 | tf_op jit(solution)/shard_map/ppermute | solution.py:15
  58.1 9.0 %collective-permute-start.9 = (f32[128,256]{0,1:T(8,128)S(1)}, f32[128,256]{0,1:T(8,128)S(1)}, u32[]{:S(2)}, u32[]{:S(2)}) collective-permute-start(f32[128,256]{0,1:T(8,128)S(1)} %collective-permute-done.7), channel_id=1, source_target_pairs={{0,15},{1,0},{2,1},{3,2},{4,3},{5,4},{6,5},{7,6},{8,7},{9,8},{10,9... | collective-permute-start | bytes 393224 | tf_op jit(solution)/shard_map/ppermute | solution.py:18
  62.5 9.0 %collective-permute-start.8 = (f32[128,256]{0,1:T(8,128)S(1)}, f32[128,256]{0,1:T(8,128)S(1)}, u32[]{:S(2)}, u32[]{:S(2)}) collective-permute-start(f32[128,256]{0,1:T(8,128)S(1)} %collective-permute-done.6), channel_id=1, source_target_pairs={{0,1},{1,2},{2,3},{3,4},{4,5},{5,6},{6,7},{7,8},{8,9},{9,10},{10,1... | collective-permute-start | bytes 393224 | tf_op jit(solution)/shard_map/ppermute | solution.py:15
  62.6 9.0 %collective-permute-start.26 = (f32[128,256]{0,1:T(8,128)S(1)}, f32[128,256]{0,1:T(8,128)S(1)}, u32[]{:S(2)}, u32[]{:S(2)}) collective-permute-start(f32[128,256]{0,1:T(8,128)S(1)} %collective-permute-done.24), channel_id=1, source_target_pairs={{0,15},{1,0},{2,1},{3,2},{4,3},{5,4},{6,5},{7,6},{8,7},{9,8},{10,9... | collective-permute-start | bytes 393224 | tf_op jit(solution)/shard_map/ppermute | solution.py:18
  67.1 9.0 %collective-permute-start.25 = (f32[128,256]{0,1:T(8,128)S(1)}, f32[128,256]{0,1:T(8,128)S(1)}, u32[]{:S(2)}, u32[]{:S(2)}) collective-permute-start(f32[128,256]{0,1:T(8,128)S(1)} %collective-permute-done.23), channel_id=1, source_target_pairs={{0,1},{1,2},{2,3},{3,4},{4,5},{5,6},{6,7},{7,8},{8,9},{9,10},{10,1... | collective-permute-start | bytes 393224 | tf_op jit(solution)/shard_map/ppermute | solution.py:15
  67.1 9.0 %collective-permute-start.11 = (f32[128,256]{0,1:T(8,128)S(1)}, f32[128,256]{0,1:T(8,128)S(1)}, u32[]{:S(2)}, u32[]{:S(2)}) collective-permute-start(f32[128,256]{0,1:T(8,128)S(1)} %collective-permute-done.9), channel_id=1, source_target_pairs={{0,15},{1,0},{2,1},{3,2},{4,3},{5,4},{6,5},{7,6},{8,7},{9,8},{10,9... | collective-permute-start | bytes 393224 | tf_op jit(solution)/shard_map/ppermute | solution.py:18
  71.6 9.0 %collective-permute-start.10 = (f32[128,256]{0,1:T(8,128)S(1)}, f32[128,256]{0,1:T(8,128)S(1)}, u32[]{:S(2)}, u32[]{:S(2)}) collective-permute-start(f32[128,256]{0,1:T(8,128)S(1)} %collective-permute-done.8), channel_id=1, source_target_pairs={{0,1},{1,2},{2,3},{3,4},{4,5},{5,6},{6,7},{7,8},{8,9},{9,10},{10,1... | collective-permute-start | bytes 393224 | tf_op jit(solution)/shard_map/ppermute | solution.py:15
  71.7 16.3 %collective-permute-start.28 = (f32[128,256]{0,1:T(8,128)S(1)}, f32[128,256]{0,1:T(8,128)S(1)}, u32[]{:S(2)}, u32[]{:S(2)}) collective-permute-start(f32[128,256]{0,1:T(8,128)S(1)} %collective-permute-done.26), channel_id=1, source_target_pairs={{0,15},{1,0},{2,1},{3,2},{4,3},{5,4},{6,5},{7,6},{8,7},{9,8},{10,9... | collective-permute-start | bytes 393224 | tf_op jit(solution)/shard_map/ppermute | solution.py:18
  76.2 11.8 %collective-permute-start.13 = (f32[128,256]{0,1:T(8,128)S(1)}, f32[128,256]{0,1:T(8,128)S(1)}, u32[]{:S(2)}, u32[]{:S(2)}) collective-permute-start(f32[128,256]{0,1:T(8,128)S(1)} %collective-permute-done.11), channel_id=1, source_target_pairs={{0,15},{1,0},{2,1},{3,2},{4,3},{5,4},{6,5},{7,6},{8,7},{9,8},{10,9... | collective-permute-start | bytes 393224 | tf_op jit(solution)/shard_map/ppermute | solution.py:18
  147.9 142.5 %reduce-scatter.17.cloned.1.call-start = ((), (), s32[]{:S(2)}) async-start(), calls=%async_computation.12 | async-start | bytes 196608 | tf_op jit(solution)/shard_map/reduce_scatter | solution.py:123
  235.5 78.4 %reduce-scatter.11.cloned.1.call-start = ((), (), s32[]{:S(2)}) async-start(), calls=%async_computation.9 | async-start | bytes 2228224 | tf_op jit(solution)/shard_map/reduce_scatter | solution.py:42
  241.8 136.4 %reduce-scatter.9.cloned.1.call-start = ((), (), s32[]{:S(2)}) async-start(), calls=%async_computation.8 | async-start | bytes 2228224 | tf_op jit(solution)/shard_map/reduce_scatter | solution.py:42
  265.2 125.0 %reduce-scatter.23.cloned.1.call-start = ((), (), s32[]{:S(2)}) async-start(), calls=%async_computation.15 | async-start | bytes 196608 | tf_op jit(solution)/shard_map/reduce_scatter | solution.py:126
  266.3 141.4 %reduce-scatter.21.cloned.1.call-start = ((), (), s32[]{:S(2)}) async-start(), calls=%async_computation.14 | async-start | bytes 786432 | tf_op jit(solution)/shard_map/reduce_scatter | solution.py:125
  268.3 156.9 %reduce-scatter.19.cloned.1.call-start = ((), (), s32[]{:S(2)}) async-start(), calls=%async_computation.13 | async-start | bytes 786432 | tf_op jit(solution)/shard_map/reduce_scatter | solution.py:124
  269.8 201.7 %reduce-scatter.13.cloned.1.call-start = ((), (), s32[]{:S(2)}) async-start(), calls=%async_computation.10 | async-start | bytes 4718592 | tf_op jit(solution)/shard_map/reduce_scatter | solution.py:121
  280.0 237.6 %reduce-scatter.15.cloned.1.call-start = ((), (), s32[]{:S(2)}) async-start(), calls=%async_computation.11 | async-start | bytes 4718592 | tf_op jit(solution)/shard_map/reduce_scatter | solution.py:122
  (24 other events, 746.2 us)
Sparse Core Ops, SparseCore 0:
  23.2 90.9 all-reduce.6
  148.0 85.6 all-reduce.4
  236.5 12.0 reduce-scatter.16
  252.1 61.7 reduce-scatter.10
  317.5 60.6 reduce-scatter.8
  380.9 9.2 reduce-scatter.22
  393.0 14.6 reduce-scatter.20
  410.5 14.6 reduce-scatter.18
  428.0 43.4 reduce-scatter.12
  474.2 43.4 reduce-scatter.14
